TPU v7x, 32 devices: a whole 2x2x4 slice. The times are simulated.
32 devices in a mesh: groups: 2 (over x), tile: 16 (over z, y, core).
Axes of the slice: x: 2, y: 2, z: 4, core: 2. Of those that a mesh axis runs over, the one named last changes fastest.
Arguments:
- exposures: float32 [32, 8, 256, 256], P(('groups', 'tile')), parts along dimension 0, may hold values from -2400 to 2400
- row_taps: bfloat16 [5, 21], replicated, may hold values from -1.25 to 1.25
- col_taps: bfloat16 [5, 21], replicated, may hold values from -1.25 to 1.25
- kernel_coeffs: float32 [32, 8, 25, 6], P(('groups', 'tile')), parts along dimension 0, may hold values from -1.25 to 1.25
- subpixel: float32 [32, 8, 2], P(('groups', 'tile')), parts along dimension 0, may hold values from 0.1 to 0.9
- destination: int32 [32, 32], P('groups'), parts along dimension 0, may hold values from 0 to 63, as said below
Outputs:
- significance: float32 [32, 8, 4, 128, 128], P(('groups', 'tile')), parts along dimension 0
There are 2 independent parts, one for each index of `groups`. A program takes and returns all parts, laid end to end along the dimension named above; an argument that names none is the same for every part. Nothing has to cross between parts.
Inputs may be any that keep to these rules, and one draw needn't show every extreme that they name: `destination`: entry [t, v * 4 + i] is the sky slot of block i of visit v of tile t; the slots o * 4 to (o + 1) * 4 - 1 are the patches of tile index o. Of the blocks of the 1 tiles of one tile index, at most 2 name slots of one tile index, and in every draw some tile index receives exactly 2 blocks from every tile index.
All inputs are finite; a program needn't handle non-finite values.
Results may differ from a plain program's by a relative error of at most 0.0062.
Values sent between devices are 32-bit elements; how exact they have to be, the bound alone decides.
No kernel may reach another device: no remote copies, remote signals or barrier semaphores. Data moves between devices by JAX's collectives and lax.ppermute only.
A program may use at most 128 MiB of HBM per device.

v0:
```python
import jax
import jax.numpy as jnp
from jax import lax
from jax.sharding import PartitionSpec as P

BLOCK = 128
highest = lax.Precision.HIGHEST


def banded(filter_taps, length):
    tap_count = filter_taps.shape[1]
    middle = tap_count // 2
    pixels = jnp.arange(length, dtype=jnp.int32)
    offset = pixels[None, :] - pixels[:, None] + middle
    selector = (offset[:, :, None] == jnp.arange(tap_count, dtype=jnp.int32)[None, None, :]).astype(
        jnp.bfloat16
    )
    matrix = jnp.einsum("pqk,fk->fpq", selector, filter_taps, preferred_element_type=jnp.float32)
    return matrix.astype(jnp.bfloat16)


def monomials(length):
    coordinate = 2.0 * jnp.arange(length, dtype=jnp.float32) / (length - 1) - 1.0
    unity = jnp.ones((length, length), jnp.float32)
    along_rows = coordinate[:, None] * unity
    along_cols = coordinate[None, :] * unity
    return jnp.stack(
        [
            unity,
            along_rows,
            along_cols,
            along_rows * along_rows,
            along_rows * along_cols,
            along_cols * along_cols,
        ]
    )


def match_one(picture, coeffs, row_stack, col_stack, mono_maps):
    length = picture.shape[0]
    filters = col_stack.shape[0] // length
    smooth = jnp.dot(
        picture.astype(jnp.bfloat16), row_stack, preferred_element_type=jnp.float32
    ).astype(jnp.bfloat16)
    basis_maps = jnp.dot(col_stack, smooth, preferred_element_type=jnp.float32)
    basis_maps = basis_maps.reshape(filters, length, filters, length)
    poly_maps = jnp.einsum(
        "aybx,abj->jyx", basis_maps, coeffs.reshape(filters, filters, -1), precision=highest
    )
    return jnp.sum(mono_maps * poly_maps, axis=0)


def lanczos_matrix(offset_px, block_side):
    pixels = jnp.arange(block_side, dtype=jnp.float32)
    distance = pixels[:, None] - pixels[None, :] + offset_px[..., None, None]
    kernel = jnp.sinc(distance) * jnp.sinc(distance / 3.0)
    return jnp.where(jnp.abs(distance) < 3.0, kernel, 0.0)


def warp_blocks(blocks, shifts):
    block_side = blocks.shape[-1]
    vertical = lanczos_matrix(shifts[..., 0], block_side)
    horizontal = lanczos_matrix(shifts[..., 1], block_side)
    partial_value = jnp.einsum("...ji,...ik->...jk", vertical, blocks, precision=highest)
    return jnp.einsum("...jk,...lk->...jl", partial_value, horizontal, precision=highest)


def lookup(table, index):
    visit_hits = (index[..., None] == jnp.arange(table.shape[0], dtype=jnp.int32)).astype(
        table.dtype
    )
    return jnp.sum(visit_hits * table, axis=-1)


def assemble(contrib, in_slot, in_weight, owned):
    select = (jnp.arange(owned, dtype=jnp.int32)[:, None] == in_slot[None, :]).astype(
        jnp.float32
    ) * in_weight[None, :]
    numerator = jnp.dot(select, contrib, precision=highest, preferred_element_type=jnp.float32)
    denominator = jnp.sum(select, axis=1)
    return numerator / jnp.where(denominator > 0, denominator, 1.0)[:, None]


def per_device(exposures, row_taps, col_taps, kernel_coeffs, subpixel, destination):
    tile_count, visits, length = (exposures.shape[0], exposures.shape[1], exposures.shape[2])
    filters = row_taps.shape[0]
    devices = lax.axis_size("tile")
    own_index = lax.axis_index("tile")
    block_side = BLOCK
    per_side = length // block_side
    block_count = per_side * per_side
    owned = tile_count * block_count
    per_dev = tile_count * visits * block_count
    capacity = 2 * tile_count
    row_stack = jnp.transpose(banded(row_taps, length), (2, 0, 1)).reshape(length, filters * length)
    col_stack = banded(col_taps, length).reshape(filters * length, length)
    mono_maps = monomials(length)
    images = exposures.reshape(tile_count * visits, length, length)
    coeffs = kernel_coeffs.reshape(tile_count * visits, filters * filters, -1)
    matched = lax.map(
        lambda packed: match_one(packed[0], packed[1], row_stack, col_stack, mono_maps),
        (images, coeffs),
    )
    power_sum = jnp.sum((matched * matched).reshape(tile_count, visits, -1), axis=(0, 2))
    power_all = lax.psum(power_sum, "tile")
    variance = power_all / (tile_count * devices * length * length) + 1e-05
    blocks = matched.reshape(tile_count * visits, per_side, block_side, per_side, block_side)
    blocks = blocks.transpose(0, 1, 3, 2, 4).reshape(per_dev, block_side, block_side)
    shifts = jnp.repeat(subpixel.reshape(tile_count * visits, 2), block_count, axis=0)
    local_dest = lax.dynamic_slice_in_dim(
        destination, own_index * tile_count, tile_count, 0
    ).reshape(per_dev)
    local_visit = jnp.arange(per_dev, dtype=jnp.int32) // block_count % visits
    local_scale = jnp.sqrt(lookup(variance, local_visit))
    local_owner = local_dest // owned
    owner_hits = (local_owner[:, None] == jnp.arange(devices, dtype=jnp.int32)[None, :]).astype(
        jnp.int32
    )
    block_rank = jnp.sum((jnp.cumsum(owner_hits, axis=0) - 1) * owner_hits, axis=1)
    position = local_owner * capacity + block_rank
    send_order = (
        jnp.full((devices * capacity,), per_dev, jnp.int32)
        .at[position]
        .set(jnp.arange(per_dev, dtype=jnp.int32))
    )
    is_mine = (destination // owned == own_index).astype(jnp.int32)
    arrival = jnp.cumsum(is_mine, axis=1) - 1
    chosen = is_mine[:, None, :] * (
        arrival[:, None, :] == jnp.arange(capacity, dtype=jnp.int32)[None, :, None]
    ).astype(jnp.int32)
    filled = jnp.sum(chosen, axis=2).reshape(-1)
    in_slot = jnp.sum(chosen * (destination % owned)[:, None, :], axis=2).reshape(-1)
    in_visit = jnp.sum(chosen * local_visit[None, None, :], axis=2).reshape(-1)
    in_weight = filled.astype(jnp.float32) / lookup(variance, in_visit)
    warped_own = warp_blocks(blocks, shifts)
    padded = jnp.concatenate(
        [warped_own, jnp.zeros((1, block_side, block_side), jnp.float32)], axis=0
    )
    outgoing = jnp.take(padded, send_order, axis=0).reshape(
        devices, capacity, block_side, block_side
    )
    arrived = lax.all_to_all(outgoing, "tile", split_axis=0, concat_axis=0, tiled=True)
    template = assemble(
        arrived.reshape(devices * capacity, block_side * block_side), in_slot, in_weight, owned
    )
    at_slots = jnp.take(template, in_slot, axis=0).reshape(
        devices, capacity, block_side, block_side
    )
    returned = lax.all_to_all(at_slots, "tile", split_axis=0, concat_axis=0, tiled=True)
    mine_back = jnp.take(
        returned.reshape(devices * capacity, block_side, block_side), position, axis=0
    )
    result = (warped_own - mine_back) / local_scale[:, None, None]
    return result.reshape(tile_count, visits, block_count, block_side, block_side)


def solution(mesh):
    return jax.shard_map(
        per_device,
        mesh=mesh,
        in_specs=(
            P(("groups", "tile"), None, None, None),
            P(),
            P(),
            P(("groups", "tile"), None, None, None),
            P(("groups", "tile"), None, None),
            P("groups", None),
        ),
        out_specs=P(("groups", "tile"), None, None, None, None),
        check_vma=False,
    )
```

profile of v0, /device:TPU:13, one launch (start us, length us, event | category | flops | bytes accessed | tf_op | source)
XLA Modules:
  0.0 478.9 jit_solution(7830950791814079655)
XLA Ops:
  3.3 2.7 bitcast_convert_fusion
  14.9 4.9 %stack.24 = f32[6,256,256]{2,0,1:T(8,128)S(1)} concatenate(f32[1,256,256]{2,0,1:T(1,128)} %stack_broadcast_in_dim.3, f32[1,256,256]{2,0,1:T(1,128)} %stack.20, f32[1,256,256]{2,0,1:T(1,128)} %stack.21, f32[1,256,256]{2,0,1:T(1,128)} %stack.22, f32[1,256,256]{2,0,1:T(1,128)} %broadcast_multiply_fusion, f32[1,256,256]{2,0,1:T(1,128)} %stack.23), dimensions={0} | concatenate | bytes 3145728 | tf_op jit(solution)/shard_map/stack | solution.py:27
  19.8 290.9 %while.10 = (s32[]{:T(128)}, f32[8,256,256]{2,1,0:T(8,128)}, f32[8,25,6]{1,2,0:T(8,128)S(1)}, bf16[8,256,256]{2,1,0:T(8,128)(2,1)}, bf16[256,1280]{1,0:T(8,128)(...) while((s32[]{:T(128)}, f32[8,256,256]{2,1,0:T(8,128)}, ...), condition=%wide.region_2.4_spmd, body=%wide.region_0.3_spmd.sunk | while | flops 1125646336 | bytes 43125792 | solution.py:100
  19.8 5.0 %convolution_bitcast_fusion.2 = f32[1280,1280]{0,1:T(8,128)} fusion(bf16[1280,256]{1,0:T(8,128)(2,1)S(1)} %get-tuple-element.152, bf16[256,1280]{1,0:T(8,128)(2,1)S(1)} %get-tuple-element.151, bf16[8,256,256]{2,1,0:T(8,128)(2,1)} %get-tuple-element.150, s32[]{:T(128)S(6)} %copy.58), kind=kOutput, calls=%fused_computation.4.clone.1 | convolution fusion | flops 1006960640 | bytes 7995396 | tf_op jit(solution)/shard_map/while/body/eval_jaxpr/dot_general | solution.py:45
  24.7 9.1 %reshape.421 = f32[5,256,5,256]{1,0,3,2:T(8,128)} reshape(f32[1280,1280]{0,1:T(8,128)} %convolution_bitcast_fusion.2) | data formatting | bytes 13107200 | tf_op jit(solution)/shard_map/while/body/eval_jaxpr/reshape | solution.py:46
  33.9 9.3 %copy.54 = f32[5,256,5,256]{3,2,0,1:T(8,128)} copy(f32[5,256,5,256]{1,0,3,2:T(8,128)} %reshape.421) | data formatting | bytes 13107200 | tf_op jit(solution)/shard_map/while/body/eval_jaxpr/reshape | solution.py:46
  43.2 12.2 %fusion.248 = f32[256,256]{1,0:T(8,128)S(1)} fusion(f32[6,256,256]{2,0,1:T(8,128)S(1)} %get-tuple-element.153, f32[5,256,5,256]{3,2,0,1:T(8,128)} %copy.54, f32[5,5,6]{1,0,2:T(8,128)S(1)} %reshape.422), kind=kOutput, calls=%fused_computation.7.clone.1 | convolution fusion | flops 118685696 | bytes 8389208 | tf_op jit(solution)/shard_map/while/body/eval_jaxpr/aybx,abj->jyx/dot_general | solution.py:47
  56.1 4.9 %convolution_bitcast_fusion.2 = f32[1280,1280]{0,1:T(8,128)} fusion(bf16[1280,256]{1,0:T(8,128)(2,1)S(1)} %get-tuple-element.152, bf16[256,1280]{1,0:T(8,128)(2,1)S(1)} %get-tuple-element.151, bf16[8,256,256]{2,1,0:T(8,128)(2,1)} %get-tuple-element.150, s32[]{:T(128)S(6)} %copy.58), kind=kOutput, calls=%fused_computation.4.clone.1 | convolution fusion | flops 1006960640 | bytes 7995396 | tf_op jit(solution)/shard_map/while/body/eval_jaxpr/dot_general | solution.py:45
  61.1 9.1 %reshape.421 = f32[5,256,5,256]{1,0,3,2:T(8,128)} reshape(f32[1280,1280]{0,1:T(8,128)} %convolution_bitcast_fusion.2) | data formatting | bytes 13107200 | tf_op jit(solution)/shard_map/while/body/eval_jaxpr/reshape | solution.py:46
  70.2 9.3 %copy.54 = f32[5,256,5,256]{3,2,0,1:T(8,128)} copy(f32[5,256,5,256]{1,0,3,2:T(8,128)} %reshape.421) | data formatting | bytes 13107200 | tf_op jit(solution)/shard_map/while/body/eval_jaxpr/reshape | solution.py:46
  79.6 12.2 %fusion.248 = f32[256,256]{1,0:T(8,128)S(1)} fusion(f32[6,256,256]{2,0,1:T(8,128)S(1)} %get-tuple-element.153, f32[5,256,5,256]{3,2,0,1:T(8,128)} %copy.54, f32[5,5,6]{1,0,2:T(8,128)S(1)} %reshape.422), kind=kOutput, calls=%fused_computation.7.clone.1 | convolution fusion | flops 118685696 | bytes 8389208 | tf_op jit(solution)/shard_map/while/body/eval_jaxpr/aybx,abj->jyx/dot_general | solution.py:47
  92.5 4.9 %convolution_bitcast_fusion.2 = f32[1280,1280]{0,1:T(8,128)} fusion(bf16[1280,256]{1,0:T(8,128)(2,1)S(1)} %get-tuple-element.152, bf16[256,1280]{1,0:T(8,128)(2,1)S(1)} %get-tuple-element.151, bf16[8,256,256]{2,1,0:T(8,128)(2,1)} %get-tuple-element.150, s32[]{:T(128)S(6)} %copy.58), kind=kOutput, calls=%fused_computation.4.clone.1 | convolution fusion | flops 1006960640 | bytes 7995396 | tf_op jit(solution)/shard_map/while/body/eval_jaxpr/dot_general | solution.py:45
  97.4 9.1 %reshape.421 = f32[5,256,5,256]{1,0,3,2:T(8,128)} reshape(f32[1280,1280]{0,1:T(8,128)} %convolution_bitcast_fusion.2) | data formatting | bytes 13107200 | tf_op jit(solution)/shard_map/while/body/eval_jaxpr/reshape | solution.py:46
  106.6 9.3 %copy.54 = f32[5,256,5,256]{3,2,0,1:T(8,128)} copy(f32[5,256,5,256]{1,0,3,2:T(8,128)} %reshape.421) | data formatting | bytes 13107200 | tf_op jit(solution)/shard_map/while/body/eval_jaxpr/reshape | solution.py:46
  115.9 12.2 %fusion.248 = f32[256,256]{1,0:T(8,128)S(1)} fusion(f32[6,256,256]{2,0,1:T(8,128)S(1)} %get-tuple-element.153, f32[5,256,5,256]{3,2,0,1:T(8,128)} %copy.54, f32[5,5,6]{1,0,2:T(8,128)S(1)} %reshape.422), kind=kOutput, calls=%fused_computation.7.clone.1 | convolution fusion | flops 118685696 | bytes 8389208 | tf_op jit(solution)/shard_map/while/body/eval_jaxpr/aybx,abj->jyx/dot_general | solution.py:47
  128.8 4.9 %convolution_bitcast_fusion.2 = f32[1280,1280]{0,1:T(8,128)} fusion(bf16[1280,256]{1,0:T(8,128)(2,1)S(1)} %get-tuple-element.152, bf16[256,1280]{1,0:T(8,128)(2,1)S(1)} %get-tuple-element.151, bf16[8,256,256]{2,1,0:T(8,128)(2,1)} %get-tuple-element.150, s32[]{:T(128)S(6)} %copy.58), kind=kOutput, calls=%fused_computation.4.clone.1 | convolution fusion | flops 1006960640 | bytes 7995396 | tf_op jit(solution)/shard_map/while/body/eval_jaxpr/dot_general | solution.py:45
  133.8 9.1 %reshape.421 = f32[5,256,5,256]{1,0,3,2:T(8,128)} reshape(f32[1280,1280]{0,1:T(8,128)} %convolution_bitcast_fusion.2) | data formatting | bytes 13107200 | tf_op jit(solution)/shard_map/while/body/eval_jaxpr/reshape | solution.py:46
  142.9 9.3 %copy.54 = f32[5,256,5,256]{3,2,0,1:T(8,128)} copy(f32[5,256,5,256]{1,0,3,2:T(8,128)} %reshape.421) | data formatting | bytes 13107200 | tf_op jit(solution)/shard_map/while/body/eval_jaxpr/reshape | solution.py:46
  152.3 12.2 %fusion.248 = f32[256,256]{1,0:T(8,128)S(1)} fusion(f32[6,256,256]{2,0,1:T(8,128)S(1)} %get-tuple-element.153, f32[5,256,5,256]{3,2,0,1:T(8,128)} %copy.54, f32[5,5,6]{1,0,2:T(8,128)S(1)} %reshape.422), kind=kOutput, calls=%fused_computation.7.clone.1 | convolution fusion | flops 118685696 | bytes 8389208 | tf_op jit(solution)/shard_map/while/body/eval_jaxpr/aybx,abj->jyx/dot_general | solution.py:47
  165.2 4.9 %convolution_bitcast_fusion.2 = f32[1280,1280]{0,1:T(8,128)} fusion(bf16[1280,256]{1,0:T(8,128)(2,1)S(1)} %get-tuple-element.152, bf16[256,1280]{1,0:T(8,128)(2,1)S(1)} %get-tuple-element.151, bf16[8,256,256]{2,1,0:T(8,128)(2,1)} %get-tuple-element.150, s32[]{:T(128)S(6)} %copy.58), kind=kOutput, calls=%fused_computation.4.clone.1 | convolution fusion | flops 1006960640 | bytes 7995396 | tf_op jit(solution)/shard_map/while/body/eval_jaxpr/dot_general | solution.py:45
  170.2 9.1 %reshape.421 = f32[5,256,5,256]{1,0,3,2:T(8,128)} reshape(f32[1280,1280]{0,1:T(8,128)} %convolution_bitcast_fusion.2) | data formatting | bytes 13107200 | tf_op jit(solution)/shard_map/while/body/eval_jaxpr/reshape | solution.py:46
  179.3 9.3 %copy.54 = f32[5,256,5,256]{3,2,0,1:T(8,128)} copy(f32[5,256,5,256]{1,0,3,2:T(8,128)} %reshape.421) | data formatting | bytes 13107200 | tf_op jit(solution)/shard_map/while/body/eval_jaxpr/reshape | solution.py:46
  188.6 12.2 %fusion.248 = f32[256,256]{1,0:T(8,128)S(1)} fusion(f32[6,256,256]{2,0,1:T(8,128)S(1)} %get-tuple-element.153, f32[5,256,5,256]{3,2,0,1:T(8,128)} %copy.54, f32[5,5,6]{1,0,2:T(8,128)S(1)} %reshape.422), kind=kOutput, calls=%fused_computation.7.clone.1 | convolution fusion | flops 118685696 | bytes 8389208 | tf_op jit(solution)/shard_map/while/body/eval_jaxpr/aybx,abj->jyx/dot_general | solution.py:47
  201.6 4.9 %convolution_bitcast_fusion.2 = f32[1280,1280]{0,1:T(8,128)} fusion(bf16[1280,256]{1,0:T(8,128)(2,1)S(1)} %get-tuple-element.152, bf16[256,1280]{1,0:T(8,128)(2,1)S(1)} %get-tuple-element.151, bf16[8,256,256]{2,1,0:T(8,128)(2,1)} %get-tuple-element.150, s32[]{:T(128)S(6)} %copy.58), kind=kOutput, calls=%fused_computation.4.clone.1 | convolution fusion | flops 1006960640 | bytes 7995396 | tf_op jit(solution)/shard_map/while/body/eval_jaxpr/dot_general | solution.py:45
  206.5 9.1 %reshape.421 = f32[5,256,5,256]{1,0,3,2:T(8,128)} reshape(f32[1280,1280]{0,1:T(8,128)} %convolution_bitcast_fusion.2) | data formatting | bytes 13107200 | tf_op jit(solution)/shard_map/while/body/eval_jaxpr/reshape | solution.py:46
  215.6 9.3 %copy.54 = f32[5,256,5,256]{3,2,0,1:T(8,128)} copy(f32[5,256,5,256]{1,0,3,2:T(8,128)} %reshape.421) | data formatting | bytes 13107200 | tf_op jit(solution)/shard_map/while/body/eval_jaxpr/reshape | solution.py:46
  225.0 12.2 %fusion.248 = f32[256,256]{1,0:T(8,128)S(1)} fusion(f32[6,256,256]{2,0,1:T(8,128)S(1)} %get-tuple-element.153, f32[5,256,5,256]{3,2,0,1:T(8,128)} %copy.54, f32[5,5,6]{1,0,2:T(8,128)S(1)} %reshape.422), kind=kOutput, calls=%fused_computation.7.clone.1 | convolution fusion | flops 118685696 | bytes 8389208 | tf_op jit(solution)/shard_map/while/body/eval_jaxpr/aybx,abj->jyx/dot_general | solution.py:47
  237.9 4.9 %convolution_bitcast_fusion.2 = f32[1280,1280]{0,1:T(8,128)} fusion(bf16[1280,256]{1,0:T(8,128)(2,1)S(1)} %get-tuple-element.152, bf16[256,1280]{1,0:T(8,128)(2,1)S(1)} %get-tuple-element.151, bf16[8,256,256]{2,1,0:T(8,128)(2,1)} %get-tuple-element.150, s32[]{:T(128)S(6)} %copy.58), kind=kOutput, calls=%fused_computation.4.clone.1 | convolution fusion | flops 1006960640 | bytes 7995396 | tf_op jit(solution)/shard_map/while/body/eval_jaxpr/dot_general | solution.py:45
  242.9 9.1 %reshape.421 = f32[5,256,5,256]{1,0,3,2:T(8,128)} reshape(f32[1280,1280]{0,1:T(8,128)} %convolution_bitcast_fusion.2) | data formatting | bytes 13107200 | tf_op jit(solution)/shard_map/while/body/eval_jaxpr/reshape | solution.py:46
  252.0 9.3 %copy.54 = f32[5,256,5,256]{3,2,0,1:T(8,128)} copy(f32[5,256,5,256]{1,0,3,2:T(8,128)} %reshape.421) | data formatting | bytes 13107200 | tf_op jit(solution)/shard_map/while/body/eval_jaxpr/reshape | solution.py:46
  261.3 12.2 %fusion.248 = f32[256,256]{1,0:T(8,128)S(1)} fusion(f32[6,256,256]{2,0,1:T(8,128)S(1)} %get-tuple-element.153, f32[5,256,5,256]{3,2,0,1:T(8,128)} %copy.54, f32[5,5,6]{1,0,2:T(8,128)S(1)} %reshape.422), kind=kOutput, calls=%fused_computation.7.clone.1 | convolution fusion | flops 118685696 | bytes 8389208 | tf_op jit(solution)/shard_map/while/body/eval_jaxpr/aybx,abj->jyx/dot_general | solution.py:47
  274.3 4.9 %convolution_bitcast_fusion.2 = f32[1280,1280]{0,1:T(8,128)} fusion(bf16[1280,256]{1,0:T(8,128)(2,1)S(1)} %get-tuple-element.152, bf16[256,1280]{1,0:T(8,128)(2,1)S(1)} %get-tuple-element.151, bf16[8,256,256]{2,1,0:T(8,128)(2,1)} %get-tuple-element.150, s32[]{:T(128)S(6)} %copy.58), kind=kOutput, calls=%fused_computation.4.clone.1 | convolution fusion | flops 1006960640 | bytes 7995396 | tf_op jit(solution)/shard_map/while/body/eval_jaxpr/dot_general | solution.py:45
  279.2 9.1 %reshape.421 = f32[5,256,5,256]{1,0,3,2:T(8,128)} reshape(f32[1280,1280]{0,1:T(8,128)} %convolution_bitcast_fusion.2) | data formatting | bytes 13107200 | tf_op jit(solution)/shard_map/while/body/eval_jaxpr/reshape | solution.py:46
  288.4 9.3 %copy.54 = f32[5,256,5,256]{3,2,0,1:T(8,128)} copy(f32[5,256,5,256]{1,0,3,2:T(8,128)} %reshape.421) | data formatting | bytes 13107200 | tf_op jit(solution)/shard_map/while/body/eval_jaxpr/reshape | solution.py:46
  297.7 12.2 %fusion.248 = f32[256,256]{1,0:T(8,128)S(1)} fusion(f32[6,256,256]{2,0,1:T(8,128)S(1)} %get-tuple-element.153, f32[5,256,5,256]{3,2,0,1:T(8,128)} %copy.54, f32[5,5,6]{1,0,2:T(8,128)S(1)} %reshape.422), kind=kOutput, calls=%fused_computation.7.clone.1 | convolution fusion | flops 118685696 | bytes 8389208 | tf_op jit(solution)/shard_map/while/body/eval_jaxpr/aybx,abj->jyx/dot_general | solution.py:47
  310.6 2.3 reshape.370
  314.8 9.1 %fusion.42 = f32[32,128,128]{2,1,0:T(8,128)S(1)} fusion(f32[32,128,128]{2,1,0:T(8,128)} %bitcast.114, f32[32]{0:T(128)S(1)} %get-tuple-element.85, f32[128,128]{1,0:T(8,128)S(1)} %iota_subtract_fusion), kind=kOutput, calls=%fused_computation.71 | convolution fusion | flops 842530816 | bytes 4259968 | tf_op jit(solution)/shard_map/...ji,...ik->...jk/dot_general | solution.py:64
  324.0 9.2 %fusion.51 = f32[32,128,128]{2,1,0:T(8,128)S(1)} fusion(f32[32,128,128]{2,1,0:T(8,128)S(1)} %fusion.42, f32[32]{0:T(128)S(1)} %get-tuple-element.84, f32[128,128]{1,0:T(8,128)S(1)} %iota_subtract_fusion), kind=kOutput, calls=%fused_computation.78 | convolution fusion | flops 842530816 | bytes 4259968 | tf_op jit(solution)/shard_map/...jk,...lk->...jl/dot_general | solution.py:65
  334.8 2.0 gather_fusion
  336.8 3.1 broadcast_select_fusion.1
  339.9 6.5 %all-to-all-start = ((f32[16,2,128,128]{3,2,1,0:T(8,128)}), f32[16,2,128,128]{3,2,1,0:T(8,128)S(1)}, u32[]{:S(2)}, u32[]{:S(2)}) async-start(f32[16,2,128,128]{3,2,1,0:T(8,128)} %broadcast_select_fusion.1), calls=%async_computation | async-start | bytes 4194304 | tf_op jit(solution)/shard_map/all_to_all | solution.py:142
  346.4 1.9 multiply_reduce_fusion
  348.3 62.1 %psum.7 = f32[8]{0:T(128)S(1)} all-reduce(f32[8]{0:T(128)S(1)} %multiply_reduce_fusion), channel_id=1, replica_groups=mesh['groups'=2,'tile'=16] {'tile'}, use_global_device_ids=true, to_apply=%region_10.12 | all-reduce | flops 8 | bytes 64 | tf_op jit(solution)/shard_map/psum | solution.py:105
  411.8 2.2 convolution_divide_fusion
  417.2 5.9 %all-to-all-start.1 = ((f32[16,2,128,128]{3,2,1,0:T(8,128)}), f32[16,2,128,128]{3,2,1,0:T(8,128)S(1)}, u32[]{:S(2)}, u32[]{:S(2)}) async-start(f32[16,2,128,128]{3,2,1,0:T(8,128)} %broadcast_select_fusion), calls=%async_computation.1 | async-start | bytes 4194304 | tf_op jit(solution)/shard_map/all_to_all | solution.py:149
  423.2 47.4 %all-to-all-done.1 = f32[16,2,128,128]{3,2,1,0:T(8,128)S(1)} async-done(((f32[16,2,128,128]{3,2,1,0:T(8,128)}), f32[16,2,128,128]{3,2,1,0:T(8,128)S(1)}, u32[]{:S(2)}, u32[]{:S(2)}) %all-to-all-start.1) | async-done | bytes 2097184 | tf_op jit(solution)/shard_map/all_to_all | solution.py:149
  471.9 3.7 gather_fusion.2
  475.6 3.3 subtract_divide_fusion
  (102 shorter events, 27.9 us)
Async XLA Ops:
  0.0 6.0 %copy-start = (bf16[5,21]{1,0:T(8,128)(2,1)S(1)}, bf16[5,21]{1,0:T(8,128)(2,1)}, u32[]{:S(2)}) copy-start(bf16[5,21]{1,0:T(8,128)(2,1)} %param.10) | copy-start | bytes 634
  6.0 1.8 copy-start.7
  312.9 1.6 copy-start.6
  333.2 1.4 copy-start.2
  339.9 71.9 %all-to-all-start = ((f32[16,2,128,128]{3,2,1,0:T(8,128)}), f32[16,2,128,128]{3,2,1,0:T(8,128)S(1)}, u32[]{:S(2)}, u32[]{:S(2)}) async-start(f32[16,2,128,128]{3,2,1,0:T(8,128)} %broadcast_select_fusion.1), calls=%async_computation | async-start | bytes 4194304 | tf_op jit(solution)/shard_map/all_to_all | solution.py:142
  346.4 64.0 %copy-start.5 = (s32[16,32]{1,0:T(8,128)S(1)}, s32[16,32]{1,0:T(8,128)}, u32[]{:S(2)}) copy-start(s32[16,32]{1,0:T(8,128)} %param.14) | copy-start | bytes 6148
  417.2 53.3 %all-to-all-start.1 = ((f32[16,2,128,128]{3,2,1,0:T(8,128)}), f32[16,2,128,128]{3,2,1,0:T(8,128)S(1)}, u32[]{:S(2)}, u32[]{:S(2)}) async-start(f32[16,2,128,128]{3,2,1,0:T(8,128)} %broadcast_select_fusion), calls=%async_computation.1 | async-start | bytes 4194304 | tf_op jit(solution)/shard_map/all_to_all | solution.py:149
  470.6 1.3 copy-start.4
  471.9 3.7 copy-start.3
  471.9 7.0 %copy-start.1 = (bf16[5,21]{1,0:T(8,128)(2,1)S(1)}, bf16[5,21]{1,0:T(8,128)(2,1)}, u32[]{:S(2)}) copy-start(bf16[5,21]{1,0:T(8,128)(2,1)} %param.10) | copy-start | bytes 634
where the time goes:
time: 482 us; the launch traced here: 479 us
  local copies, waits for them, and re-layouts  180 us (37%)
  matrix products  160 us (33%)
  blocking collectives  62.1 us (13%)
  waiting for transfers between devices  47.4 us (10%)
  other arithmetic  16 us (3%)
  starting transfers between devices  12.5 us (3%)
    reshape x16, local copies, waits for them, and re-layouts, match_one(): basis_maps = basis_maps.reshape(filters, length, filters, length)  147 us
    dot_general x8, matrix products, match_one(): jnp.einsum('aybx,abj->jyx', basis_maps, coeffs.reshape(filters, filters,...  97.6 us
    psum x1, blocking collectives, per_device(): power_all = lax.psum(power_sum, 'tile')  62.1 us
    all_to_all x1, waiting for transfers between devices, per_device(): lax.all_to_all(at_slots, 'tile', split_axis=0, concat_axis=0, tiled=True)  47.4 us
    dot_general x8, matrix products, match_one(): basis_maps = jnp.dot(col_stack, smooth, preferred_element_type=jnp.float32)  39.6 us
  transfers between devices with their start and end apart: 2, of which 1 were waited for; matrix products, arithmetic and copies ran while one was open for 1% of the time, Pallas kernels for 0%

commit v1 on v0

--- a/solution.py
+++ b/solution.py
@@ -102,7 +102,11 @@
         (images, coeffs),
     )
     power_sum = jnp.sum((matched * matched).reshape(tile_count, visits, -1), axis=(0, 2))
-    power_all = lax.psum(power_sum, "tile")
+    power_all = power_sum
+    for hop in (1, 2, 4, 8):
+        power_all = power_all + lax.ppermute(
+            power_all, "tile", [(dev, dev ^ hop) for dev in range(16)]
+        )
     variance = power_all / (tile_count * devices * length * length) + 1e-05
     blocks = matched.reshape(tile_count * visits, per_side, block_side, per_side, block_side)
     blocks = blocks.transpose(0, 1, 3, 2, 4).reshape(per_dev, block_side, block_side)

time: 482 us -> 463 us (0.961)
  blocking collectives: 62.1 us -> 0 us
  waiting for transfers between devices: 47.4 us -> 89.5 us
    psum x1 -> x0, blocking collectives: 62.1 us -> none  [per_device(): power_all = lax.psum(power_sum, 'tile')]
    ppermute x0 -> x4, waiting for transfers between devices: none -> 40.1 us  [per_device(): lax.ppermute(power_all, 'tile', [(dev, dev ^ hop) for dev in range(16)])]
  transfers between devices with their start and end apart: 2 -> 6, of which waited for: 1 -> 5; matrix products, arithmetic and copies ran while one was open for 1% -> 1% of each run, Pallas kernels for 0% -> 0%
where the time goes in v1:
time: 463 us; the launch traced here: 460 us
  local copies, waits for them, and re-layouts  180 us (39%)
  matrix products  161 us (35%)
  waiting for transfers between devices  89.5 us (19%)
  other arithmetic  15 us (3%)
  starting transfers between devices  14.1 us (3%)
    reshape x16, local copies, waits for them, and re-layouts, match_one(): basis_maps = basis_maps.reshape(filters, length, filters, length)  147 us
    dot_general x8, matrix products, match_one(): jnp.einsum('aybx,abj->jyx', basis_maps, coeffs.reshape(filters, filters,...  97.6 us
    all_to_all x1, waiting for transfers between devices, per_device(): lax.all_to_all(at_slots, 'tile', split_axis=0, concat_axis=0, tiled=True)  47.4 us
    ppermute x4, waiting for transfers between devices, per_device(): lax.ppermute(power_all, 'tile', [(dev, dev ^ hop) for dev in range(16)])  40.1 us
    dot_general x8, matrix products, match_one(): basis_maps = jnp.dot(col_stack, smooth, preferred_element_type=jnp.float32)  39.6 us
    another operation x6, local copies, waits for them, and re-layouts, monomials(): jnp.stack([unity, along_rows, along_cols, along_rows * along_rows, along_...  9.49 us
  transfers between devices with their start and end apart: 6, of which 5 were waited for; matrix products, arithmetic and copies ran while one was open for 1% of the time, Pallas kernels for 0%

profile of v1, /device:TPU:13, one launch (start us, length us, event | category | flops | bytes accessed | tf_op | source)
XLA Modules:
  0.0 460.0 jit_solution(11003813833639923636)
XLA Ops:
  6.0 2.4 fusion.154
  14.3 4.9 %stack.24 = f32[6,256,256]{2,0,1:T(8,128)S(1)} concatenate(f32[1,256,256]{2,0,1:T(1,128)} %stack_broadcast_in_dim.3, f32[1,256,256]{2,0,1:T(1,128)} %stack.20, f32[1,256,256]{2,0,1:T(1,128)} %stack.21, f32[1,256,256]{2,0,1:T(1,128)} %stack.22, f32[1,256,256]{2,0,1:T(1,128)} %broadcast_multiply_fusion, f32[1,256,256]{2,0,1:T(1,128)} %stack.23), dimensions={0} | concatenate | bytes 3145728 | tf_op jit(solution)/shard_map/stack | solution.py:27
  19.2 290.9 %while.10 = (s32[]{:T(128)}, f32[8,256,256]{2,1,0:T(8,128)}, f32[8,25,6]{1,2,0:T(8,128)S(1)}, bf16[8,256,256]{2,1,0:T(8,128)(2,1)}, bf16[256,1280]{1,0:T(8,128)(...) while((s32[]{:T(128)}, f32[8,256,256]{2,1,0:T(8,128)}, ...), condition=%wide.region_2.4_spmd, body=%wide.region_0.3_spmd.sunk | while | flops 1125646336 | bytes 43126800 | solution.py:100
  19.2 5.0 %convolution_bitcast_fusion.2 = f32[1280,1280]{0,1:T(8,128)} fusion(bf16[1280,256]{1,0:T(8,128)(2,1)S(1)} %get-tuple-element.152, bf16[256,1280]{1,0:T(8,128)(2,1)S(1)} %get-tuple-element.151, bf16[8,256,256]{2,1,0:T(8,128)(2,1)} %get-tuple-element.150, s32[]{:T(128)} %get-tuple-element.139), kind=kOutput, calls=%fused_computation.4.clone.1 | convolution fusion | flops 1006960640 | bytes 7995904 | tf_op jit(solution)/shard_map/while/body/eval_jaxpr/dot_general | solution.py:45
  24.1 9.1 %reshape.421 = f32[5,256,5,256]{1,0,3,2:T(8,128)} reshape(f32[1280,1280]{0,1:T(8,128)} %convolution_bitcast_fusion.2) | data formatting | bytes 13107200 | tf_op jit(solution)/shard_map/while/body/eval_jaxpr/reshape | solution.py:46
  33.3 9.3 %copy.54 = f32[5,256,5,256]{3,2,0,1:T(8,128)} copy(f32[5,256,5,256]{1,0,3,2:T(8,128)} %reshape.421) | data formatting | bytes 13107200 | tf_op jit(solution)/shard_map/while/body/eval_jaxpr/reshape | solution.py:46
  42.6 12.2 %fusion.248 = f32[256,256]{1,0:T(8,128)S(1)} fusion(f32[6,256,256]{2,0,1:T(8,128)S(1)} %get-tuple-element.153, f32[5,256,5,256]{3,2,0,1:T(8,128)} %copy.54, f32[5,5,6]{1,0,2:T(8,128)S(1)} %reshape.422), kind=kOutput, calls=%fused_computation.7.clone.1 | convolution fusion | flops 118685696 | bytes 8389208 | tf_op jit(solution)/shard_map/while/body/eval_jaxpr/aybx,abj->jyx/dot_general | solution.py:47
  55.5 4.9 %convolution_bitcast_fusion.2 = f32[1280,1280]{0,1:T(8,128)} fusion(bf16[1280,256]{1,0:T(8,128)(2,1)S(1)} %get-tuple-element.152, bf16[256,1280]{1,0:T(8,128)(2,1)S(1)} %get-tuple-element.151, bf16[8,256,256]{2,1,0:T(8,128)(2,1)} %get-tuple-element.150, s32[]{:T(128)} %get-tuple-element.139), kind=kOutput, calls=%fused_computation.4.clone.1 | convolution fusion | flops 1006960640 | bytes 7995904 | tf_op jit(solution)/shard_map/while/body/eval_jaxpr/dot_general | solution.py:45
  60.5 9.1 %reshape.421 = f32[5,256,5,256]{1,0,3,2:T(8,128)} reshape(f32[1280,1280]{0,1:T(8,128)} %convolution_bitcast_fusion.2) | data formatting | bytes 13107200 | tf_op jit(solution)/shard_map/while/body/eval_jaxpr/reshape | solution.py:46
  69.6 9.3 %copy.54 = f32[5,256,5,256]{3,2,0,1:T(8,128)} copy(f32[5,256,5,256]{1,0,3,2:T(8,128)} %reshape.421) | data formatting | bytes 13107200 | tf_op jit(solution)/shard_map/while/body/eval_jaxpr/reshape | solution.py:46
  79.0 12.2 %fusion.248 = f32[256,256]{1,0:T(8,128)S(1)} fusion(f32[6,256,256]{2,0,1:T(8,128)S(1)} %get-tuple-element.153, f32[5,256,5,256]{3,2,0,1:T(8,128)} %copy.54, f32[5,5,6]{1,0,2:T(8,128)S(1)} %reshape.422), kind=kOutput, calls=%fused_computation.7.clone.1 | convolution fusion | flops 118685696 | bytes 8389208 | tf_op jit(solution)/shard_map/while/body/eval_jaxpr/aybx,abj->jyx/dot_general | solution.py:47
  91.9 4.9 %convolution_bitcast_fusion.2 = f32[1280,1280]{0,1:T(8,128)} fusion(bf16[1280,256]{1,0:T(8,128)(2,1)S(1)} %get-tuple-element.152, bf16[256,1280]{1,0:T(8,128)(2,1)S(1)} %get-tuple-element.151, bf16[8,256,256]{2,1,0:T(8,128)(2,1)} %get-tuple-element.150, s32[]{:T(128)} %get-tuple-element.139), kind=kOutput, calls=%fused_computation.4.clone.1 | convolution fusion | flops 1006960640 | bytes 7995904 | tf_op jit(solution)/shard_map/while/body/eval_jaxpr/dot_general | solution.py:45
  96.8 9.1 %reshape.421 = f32[5,256,5,256]{1,0,3,2:T(8,128)} reshape(f32[1280,1280]{0,1:T(8,128)} %convolution_bitcast_fusion.2) | data formatting | bytes 13107200 | tf_op jit(solution)/shard_map/while/body/eval_jaxpr/reshape | solution.py:46
  106.0 9.3 %copy.54 = f32[5,256,5,256]{3,2,0,1:T(8,128)} copy(f32[5,256,5,256]{1,0,3,2:T(8,128)} %reshape.421) | data formatting | bytes 13107200 | tf_op jit(solution)/shard_map/while/body/eval_jaxpr/reshape | solution.py:46
  115.3 12.2 %fusion.248 = f32[256,256]{1,0:T(8,128)S(1)} fusion(f32[6,256,256]{2,0,1:T(8,128)S(1)} %get-tuple-element.153, f32[5,256,5,256]{3,2,0,1:T(8,128)} %copy.54, f32[5,5,6]{1,0,2:T(8,128)S(1)} %reshape.422), kind=kOutput, calls=%fused_computation.7.clone.1 | convolution fusion | flops 118685696 | bytes 8389208 | tf_op jit(solution)/shard_map/while/body/eval_jaxpr/aybx,abj->jyx/dot_general | solution.py:47
  128.2 4.9 %convolution_bitcast_fusion.2 = f32[1280,1280]{0,1:T(8,128)} fusion(bf16[1280,256]{1,0:T(8,128)(2,1)S(1)} %get-tuple-element.152, bf16[256,1280]{1,0:T(8,128)(2,1)S(1)} %get-tuple-element.151, bf16[8,256,256]{2,1,0:T(8,128)(2,1)} %get-tuple-element.150, s32[]{:T(128)} %get-tuple-element.139), kind=kOutput, calls=%fused_computation.4.clone.1 | convolution fusion | flops 1006960640 | bytes 7995904 | tf_op jit(solution)/shard_map/while/body/eval_jaxpr/dot_general | solution.py:45
  133.2 9.1 %reshape.421 = f32[5,256,5,256]{1,0,3,2:T(8,128)} reshape(f32[1280,1280]{0,1:T(8,128)} %convolution_bitcast_fusion.2) | data formatting | bytes 13107200 | tf_op jit(solution)/shard_map/while/body/eval_jaxpr/reshape | solution.py:46
  142.3 9.3 %copy.54 = f32[5,256,5,256]{3,2,0,1:T(8,128)} copy(f32[5,256,5,256]{1,0,3,2:T(8,128)} %reshape.421) | data formatting | bytes 13107200 | tf_op jit(solution)/shard_map/while/body/eval_jaxpr/reshape | solution.py:46
  151.7 12.2 %fusion.248 = f32[256,256]{1,0:T(8,128)S(1)} fusion(f32[6,256,256]{2,0,1:T(8,128)S(1)} %get-tuple-element.153, f32[5,256,5,256]{3,2,0,1:T(8,128)} %copy.54, f32[5,5,6]{1,0,2:T(8,128)S(1)} %reshape.422), kind=kOutput, calls=%fused_computation.7.clone.1 | convolution fusion | flops 118685696 | bytes 8389208 | tf_op jit(solution)/shard_map/while/body/eval_jaxpr/aybx,abj->jyx/dot_general | solution.py:47
  164.6 4.9 %convolution_bitcast_fusion.2 = f32[1280,1280]{0,1:T(8,128)} fusion(bf16[1280,256]{1,0:T(8,128)(2,1)S(1)} %get-tuple-element.152, bf16[256,1280]{1,0:T(8,128)(2,1)S(1)} %get-tuple-element.151, bf16[8,256,256]{2,1,0:T(8,128)(2,1)} %get-tuple-element.150, s32[]{:T(128)} %get-tuple-element.139), kind=kOutput, calls=%fused_computation.4.clone.1 | convolution fusion | flops 1006960640 | bytes 7995904 | tf_op jit(solution)/shard_map/while/body/eval_jaxpr/dot_general | solution.py:45
  169.6 9.1 %reshape.421 = f32[5,256,5,256]{1,0,3,2:T(8,128)} reshape(f32[1280,1280]{0,1:T(8,128)} %convolution_bitcast_fusion.2) | data formatting | bytes 13107200 | tf_op jit(solution)/shard_map/while/body/eval_jaxpr/reshape | solution.py:46
  178.7 9.3 %copy.54 = f32[5,256,5,256]{3,2,0,1:T(8,128)} copy(f32[5,256,5,256]{1,0,3,2:T(8,128)} %reshape.421) | data formatting | bytes 13107200 | tf_op jit(solution)/shard_map/while/body/eval_jaxpr/reshape | solution.py:46
  188.0 12.2 %fusion.248 = f32[256,256]{1,0:T(8,128)S(1)} fusion(f32[6,256,256]{2,0,1:T(8,128)S(1)} %get-tuple-element.153, f32[5,256,5,256]{3,2,0,1:T(8,128)} %copy.54, f32[5,5,6]{1,0,2:T(8,128)S(1)} %reshape.422), kind=kOutput, calls=%fused_computation.7.clone.1 | convolution fusion | flops 118685696 | bytes 8389208 | tf_op jit(solution)/shard_map/while/body/eval_jaxpr/aybx,abj->jyx/dot_general | solution.py:47
  201.0 4.9 %convolution_bitcast_fusion.2 = f32[1280,1280]{0,1:T(8,128)} fusion(bf16[1280,256]{1,0:T(8,128)(2,1)S(1)} %get-tuple-element.152, bf16[256,1280]{1,0:T(8,128)(2,1)S(1)} %get-tuple-element.151, bf16[8,256,256]{2,1,0:T(8,128)(2,1)} %get-tuple-element.150, s32[]{:T(128)} %get-tuple-element.139), kind=kOutput, calls=%fused_computation.4.clone.1 | convolution fusion | flops 1006960640 | bytes 7995904 | tf_op jit(solution)/shard_map/while/body/eval_jaxpr/dot_general | solution.py:45
  205.9 9.1 %reshape.421 = f32[5,256,5,256]{1,0,3,2:T(8,128)} reshape(f32[1280,1280]{0,1:T(8,128)} %convolution_bitcast_fusion.2) | data formatting | bytes 13107200 | tf_op jit(solution)/shard_map/while/body/eval_jaxpr/reshape | solution.py:46
  215.0 9.3 %copy.54 = f32[5,256,5,256]{3,2,0,1:T(8,128)} copy(f32[5,256,5,256]{1,0,3,2:T(8,128)} %reshape.421) | data formatting | bytes 13107200 | tf_op jit(solution)/shard_map/while/body/eval_jaxpr/reshape | solution.py:46
  224.4 12.2 %fusion.248 = f32[256,256]{1,0:T(8,128)S(1)} fusion(f32[6,256,256]{2,0,1:T(8,128)S(1)} %get-tuple-element.153, f32[5,256,5,256]{3,2,0,1:T(8,128)} %copy.54, f32[5,5,6]{1,0,2:T(8,128)S(1)} %reshape.422), kind=kOutput, calls=%fused_computation.7.clone.1 | convolution fusion | flops 118685696 | bytes 8389208 | tf_op jit(solution)/shard_map/while/body/eval_jaxpr/aybx,abj->jyx/dot_general | solution.py:47
  237.3 4.9 %convolution_bitcast_fusion.2 = f32[1280,1280]{0,1:T(8,128)} fusion(bf16[1280,256]{1,0:T(8,128)(2,1)S(1)} %get-tuple-element.152, bf16[256,1280]{1,0:T(8,128)(2,1)S(1)} %get-tuple-element.151, bf16[8,256,256]{2,1,0:T(8,128)(2,1)} %get-tuple-element.150, s32[]{:T(128)} %get-tuple-element.139), kind=kOutput, calls=%fused_computation.4.clone.1 | convolution fusion | flops 1006960640 | bytes 7995904 | tf_op jit(solution)/shard_map/while/body/eval_jaxpr/dot_general | solution.py:45
  242.3 9.1 %reshape.421 = f32[5,256,5,256]{1,0,3,2:T(8,128)} reshape(f32[1280,1280]{0,1:T(8,128)} %convolution_bitcast_fusion.2) | data formatting | bytes 13107200 | tf_op jit(solution)/shard_map/while/body/eval_jaxpr/reshape | solution.py:46
  251.4 9.3 %copy.54 = f32[5,256,5,256]{3,2,0,1:T(8,128)} copy(f32[5,256,5,256]{1,0,3,2:T(8,128)} %reshape.421) | data formatting | bytes 13107200 | tf_op jit(solution)/shard_map/while/body/eval_jaxpr/reshape | solution.py:46
  260.7 12.2 %fusion.248 = f32[256,256]{1,0:T(8,128)S(1)} fusion(f32[6,256,256]{2,0,1:T(8,128)S(1)} %get-tuple-element.153, f32[5,256,5,256]{3,2,0,1:T(8,128)} %copy.54, f32[5,5,6]{1,0,2:T(8,128)S(1)} %reshape.422), kind=kOutput, calls=%fused_computation.7.clone.1 | convolution fusion | flops 118685696 | bytes 8389208 | tf_op jit(solution)/shard_map/while/body/eval_jaxpr/aybx,abj->jyx/dot_general | solution.py:47
  273.7 4.9 %convolution_bitcast_fusion.2 = f32[1280,1280]{0,1:T(8,128)} fusion(bf16[1280,256]{1,0:T(8,128)(2,1)S(1)} %get-tuple-element.152, bf16[256,1280]{1,0:T(8,128)(2,1)S(1)} %get-tuple-element.151, bf16[8,256,256]{2,1,0:T(8,128)(2,1)} %get-tuple-element.150, s32[]{:T(128)} %get-tuple-element.139), kind=kOutput, calls=%fused_computation.4.clone.1 | convolution fusion | flops 1006960640 | bytes 7995904 | tf_op jit(solution)/shard_map/while/body/eval_jaxpr/dot_general | solution.py:45
  278.6 9.1 %reshape.421 = f32[5,256,5,256]{1,0,3,2:T(8,128)} reshape(f32[1280,1280]{0,1:T(8,128)} %convolution_bitcast_fusion.2) | data formatting | bytes 13107200 | tf_op jit(solution)/shard_map/while/body/eval_jaxpr/reshape | solution.py:46
  287.8 9.3 %copy.54 = f32[5,256,5,256]{3,2,0,1:T(8,128)} copy(f32[5,256,5,256]{1,0,3,2:T(8,128)} %reshape.421) | data formatting | bytes 13107200 | tf_op jit(solution)/shard_map/while/body/eval_jaxpr/reshape | solution.py:46
  297.1 12.2 %fusion.248 = f32[256,256]{1,0:T(8,128)S(1)} fusion(f32[6,256,256]{2,0,1:T(8,128)S(1)} %get-tuple-element.153, f32[5,256,5,256]{3,2,0,1:T(8,128)} %copy.54, f32[5,5,6]{1,0,2:T(8,128)S(1)} %reshape.422), kind=kOutput, calls=%fused_computation.7.clone.1 | convolution fusion | flops 118685696 | bytes 8389208 | tf_op jit(solution)/shard_map/while/body/eval_jaxpr/aybx,abj->jyx/dot_general | solution.py:47
  310.0 2.3 reshape.370
  314.2 9.1 %fusion.42 = f32[32,128,128]{2,1,0:T(8,128)S(1)} fusion(f32[32,128,128]{2,1,0:T(8,128)} %bitcast.114, f32[32]{0:T(128)S(1)} %get-tuple-element.85, f32[128,128]{1,0:T(8,128)S(1)} %iota_subtract_fusion), kind=kOutput, calls=%fused_computation.71 | convolution fusion | flops 842530816 | bytes 4259968 | tf_op jit(solution)/shard_map/...ji,...ik->...jk/dot_general | solution.py:64
  323.4 9.2 %fusion.51 = f32[32,128,128]{2,1,0:T(8,128)S(1)} fusion(f32[32,128,128]{2,1,0:T(8,128)S(1)} %fusion.42, f32[32]{0:T(128)S(1)} %get-tuple-element.84, f32[128,128]{1,0:T(8,128)S(1)} %iota_subtract_fusion), kind=kOutput, calls=%fused_computation.78 | convolution fusion | flops 842530816 | bytes 4259968 | tf_op jit(solution)/shard_map/...jk,...lk->...jl/dot_general | solution.py:65
  336.2 3.1 broadcast_select_fusion.1
  339.3 6.5 %all-to-all-start = ((f32[16,2,128,128]{3,2,1,0:T(8,128)}), f32[16,2,128,128]{3,2,1,0:T(8,128)S(1)}, u32[]{:S(2)}, u32[]{:S(2)}) async-start(f32[16,2,128,128]{3,2,1,0:T(8,128)} %broadcast_select_fusion.1), calls=%async_computation | async-start | bytes 4194304 | tf_op jit(solution)/shard_map/all_to_all | solution.py:146
  349.7 5.8 %collective-permute-done.1 = f32[8]{0:T(128)S(1)} collective-permute-done((f32[8]{0:T(128)S(1)}, f32[8]{0:T(128)S(1)}, u32[]{:S(2)}, u32[]{:S(2)}) %collective-permute-start.1) | collective-permute-done | bytes 64 | tf_op jit(solution)/shard_map/ppermute | solution.py:107
  355.7 25.4 %collective-permute-done.2 = f32[8]{0:T(128)S(1)} collective-permute-done((f32[8]{0:T(128)S(1)}, f32[8]{0:T(128)S(1)}, u32[]{:S(2)}, u32[]{:S(2)}) %collective-permute-start.2) | collective-permute-done | bytes 64 | tf_op jit(solution)/shard_map/ppermute | solution.py:107
  382.2 8.9 %collective-permute-done.3 = f32[8]{0:T(128)S(1)} collective-permute-done((f32[8]{0:T(128)S(1)}, f32[8]{0:T(128)S(1)}, u32[]{:S(2)}, u32[]{:S(2)}) %collective-permute-start.3) | collective-permute-done | bytes 64 | tf_op jit(solution)/shard_map/ppermute | solution.py:107
  393.3 2.2 convolution_divide_fusion
  398.7 5.6 %all-to-all-start.1 = ((f32[16,2,128,128]{3,2,1,0:T(8,128)}), f32[16,2,128,128]{3,2,1,0:T(8,128)S(1)}, u32[]{:S(2)}, u32[]{:S(2)}) async-start(f32[16,2,128,128]{3,2,1,0:T(8,128)} %broadcast_select_fusion), calls=%async_computation.1 | async-start | bytes 4194304 | tf_op jit(solution)/shard_map/all_to_all | solution.py:153
  404.3 47.4 %all-to-all-done.1 = f32[16,2,128,128]{3,2,1,0:T(8,128)S(1)} async-done(((f32[16,2,128,128]{3,2,1,0:T(8,128)}), f32[16,2,128,128]{3,2,1,0:T(8,128)S(1)}, u32[]{:S(2)}, u32[]{:S(2)}) %all-to-all-start.1) | async-done | bytes 2097184 | tf_op jit(solution)/shard_map/all_to_all | solution.py:153
  453.0 3.7 gather_fusion.2
  456.7 3.3 subtract_divide_fusion
  (120 shorter events, 35.4 us)
Async XLA Ops:
  0.0 4.2 copy-start
  0.1 5.6 %copy-start.6 = (s32[256,256]{1,0:T(8,128)}, s32[256,256]{1,0:T(8,128)S(1)}, u32[]{:S(2)}) copy-start(s32[256,256]{1,0:T(8,128)S(1)} %subtract_add_fusion) | copy-start | bytes 786436
  4.2 1.8 copy-start.11
  5.7 2.9 copy-start.5
  8.4 1.3 copy-start.8
  19.2 290.9 %copy-start.10 = (s32[32]{0:T(128)S(1)}, s32[32]{0:T(128)}, u32[]{:S(2)}) copy-start(s32[32]{0:T(128)} %compare_select_fusion.3) | copy-start | bytes 388
  312.3 1.6 copy-start.9
  332.6 1.4 copy-start.2
  339.3 54.0 %all-to-all-start = ((f32[16,2,128,128]{3,2,1,0:T(8,128)}), f32[16,2,128,128]{3,2,1,0:T(8,128)S(1)}, u32[]{:S(2)}, u32[]{:S(2)}) async-start(f32[16,2,128,128]{3,2,1,0:T(8,128)} %broadcast_select_fusion.1), calls=%async_computation | async-start | bytes 4194304 | tf_op jit(solution)/shard_map/all_to_all | solution.py:146
  345.8 2.3 copy-start.7
  347.7 1.6 collective-permute-start
  349.3 6.1 %collective-permute-start.1 = (f32[8]{0:T(128)S(1)}, f32[8]{0:T(128)S(1)}, u32[]{:S(2)}, u32[]{:S(2)}) collective-permute-start(f32[8]{0:T(128)S(1)} %add.239), channel_id=1, source_target_pairs={{0,2},{1,3},{2,0},{3,1},{4,6},{5,7},{6,4},{7,5},{8,10},{9,11},{10,... | collective-permute-start | bytes 104 | tf_op jit(solution)/shard_map/ppermute | solution.py:107
  355.4 25.7 %collective-permute-start.2 = (f32[8]{0:T(128)S(1)}, f32[8]{0:T(128)S(1)}, u32[]{:S(2)}, u32[]{:S(2)}) collective-permute-start(f32[8]{0:T(128)S(1)} %add.240), channel_id=1, source_target_pairs={{0,4},{1,5},{2,6},{3,7},{4,0},{5,1},{6,2},{7,3},{8,12},{9,13},{10,... | collective-permute-start | bytes 104 | tf_op jit(solution)/shard_map/ppermute | solution.py:107
  381.2 9.9 %collective-permute-start.3 = (f32[8]{0:T(128)S(1)}, f32[8]{0:T(128)S(1)}, u32[]{:S(2)}, u32[]{:S(2)}) collective-permute-start(f32[8]{0:T(128)S(1)} %add.241), channel_id=1, source_target_pairs={{0,8},{1,9},{2,10},{3,11},{4,12},{5,13},{6,14},{7,15},{8,0},{9,1},... | collective-permute-start | bytes 104 | tf_op jit(solution)/shard_map/ppermute | solution.py:107
  398.7 53.0 %all-to-all-start.1 = ((f32[16,2,128,128]{3,2,1,0:T(8,128)}), f32[16,2,128,128]{3,2,1,0:T(8,128)S(1)}, u32[]{:S(2)}, u32[]{:S(2)}) async-start(f32[16,2,128,128]{3,2,1,0:T(8,128)} %broadcast_select_fusion), calls=%async_computation.1 | async-start | bytes 4194304 | tf_op jit(solution)/shard_map/all_to_all | solution.py:153
  451.7 1.3 copy-start.4
  453.0 3.7 copy-start.3
  453.0 7.0 %copy-start.1 = (bf16[5,21]{1,0:T(8,128)(2,1)S(1)}, bf16[5,21]{1,0:T(8,128)(2,1)}, u32[]{:S(2)}) copy-start(bf16[5,21]{1,0:T(8,128)(2,1)} %param.10) | copy-start | bytes 634
